TPU v7x, 32 devices: a whole 2x2x4 slice. The times are simulated.
32 devices in a mesh: tm: 16 (over z, y, core), strip: 2 (over x).
Axes of the slice: x: 2, y: 2, z: 4, core: 2. Of those that a mesh axis runs over, the one named last changes fastest.
Arguments:
- forward_u: float32 [16, 128, 1024], P('tm', 'strip'), may hold values from -4 to 4
- forward_v: float32 [16, 128, 1024], P('tm', 'strip'), may hold values from -4 to 4
- permittivity: float32 [128, 1024], P('strip'), may hold values from 1 to 3
- coarse_rate: float32 [16, 128, 1024], P('tm', 'strip'), may hold values from 0.2 to 8
- modulation: float32 [32], replicated, may hold values from 0 to 0.3
- tile_map: int32 [1, 8], replicated, may hold values from 0 to 31
- start_step: int32 [16], P('tm'), may hold values from 0 to 255
Outputs:
- adjoint_u: float32 [16, 128, 1024], P('tm', 'strip')
- adjoint_v: float32 [16, 128, 1024], P('tm', 'strip')
- depth_grad: float32 [32], replicated
Inputs may be any that keep to these rules, and one draw needn't show every extreme that they name: `tile_map`: tile parameter indices. `start_step`: start steps within one period.
All inputs are finite; a program needn't handle non-finite values.
Results may differ from a plain program's by a relative error of at most 0.0003.
Values sent between devices are 32-bit elements; how exact they have to be, the bound alone decides.
A program may use at most 128 MiB of HBM per device.

v0:
```python
import jax
import jax.numpy as jnp
from jax import lax
from jax.sharding import PartitionSpec as P

TILE = 128
STEPS = 2
STENCIL = 4
PERIOD = 256
stencil_coef = (-205.0 / 72.0, 8.0 / 5.0, -1.0 / 5.0, 8.0 / 315.0, -1.0 / 560.0)
time_step = 0.4
damping_rate = 0.1


def padded_2(cells, sides, width):
    for axis, dim in sides:
        count = lax.axis_size(axis)
        ends = count - 1
        head = lax.slice_in_dim(cells, 0, width, axis=dim)
        tail = lax.slice_in_dim(cells, cells.shape[dim] - width, cells.shape[dim], axis=dim)
        cells = jnp.concatenate(
            [
                lax.ppermute(tail, axis, [(i, (i + 1) % count) for i in range(ends)]),
                cells,
                lax.ppermute(head, axis, [((i + 1) % count, i) for i in range(ends)]),
            ],
            axis=dim,
        )
    return cells


def from_behind(array, axis, by):
    length = lax.axis_size(axis)
    return lax.ppermute(array, axis, [(i, (i + by) % length) for i in range(length)])


def entering(part, axis, combine, identity, reverse):
    count = lax.axis_size(axis)
    place = lax.axis_index(axis)
    ahead = count - 1 - place if reverse else place
    gathered = jax.tree.map(lambda a: lax.all_gather(a, axis), part)
    state = jax.tree.map(lambda a, e: jnp.zeros_like(a) + jnp.asarray(e, a.dtype), part, identity)

    def one(turn, state):
        source = count - 1 - turn if reverse else turn
        return combine(
            state, jax.tree.map(lambda a: lax.dynamic_index_in_dim(a, source, 0, False), gathered)
        )

    return lax.fori_loop(0, ahead, one, state)


def laplacian_rows(padded, rim_width):
    row_count = padded.shape[0] - 2 * rim_width
    center = padded[rim_width : rim_width + row_count]
    summed = 2.0 * stencil_coef[0] * center
    for offset in range(1, 5):
        along_x = (
            padded[rim_width + offset : rim_width + offset + row_count]
            + padded[rim_width - offset : rim_width - offset + row_count]
        )
        along_y = jnp.roll(center, offset, axis=1) + jnp.roll(center, -offset, axis=1)
        summed = summed + stencil_coef[offset] * (along_x + along_y)
    return summed


def row_selector(first_row, row_count, tile_rows):
    global_rows = first_row + jnp.arange(row_count, dtype=jnp.int32)
    tile_index = global_rows // TILE
    return (tile_index[:, None] == jnp.arange(tile_rows, dtype=jnp.int32)[None, :]).astype(
        jnp.float32
    )


def rows_depth(first_row, row_count, tile_depth):
    selector = row_selector(first_row, row_count, tile_depth.shape[0])
    per_tile = jnp.dot(selector, tile_depth, precision=lax.Precision.HIGHEST)
    return jnp.repeat(per_tile, TILE, axis=1)


def compose_high(earlier, latter):
    return (latter[0] * earlier[0], latter[0][None] * earlier[1] + latter[1])


def compose_low(earlier, latter):
    return (earlier[0] * latter[0], earlier[0][None] * latter[1] + earlier[1])


def shards(forward_u, forward_v, permittivity, coarse_rate, modulation, tile_map, start_step):
    start_u = forward_u[0]
    start_v = forward_v[0]
    strip_rows = start_u.shape[0]
    strip_place = lax.axis_index("strip")
    slice_count = lax.axis_size("tm")
    selector_params = (
        tile_map[:, :, None] == jnp.arange(modulation.shape[0], dtype=jnp.int32)[None, None, :]
    ).astype(jnp.float32)
    tile_depth = jnp.sum(selector_params * modulation[None, None, :], axis=2)
    cell_depth = rows_depth(strip_place * strip_rows, strip_rows, tile_depth)
    offsets = (start_step[0] + jnp.arange(STEPS, dtype=jnp.int32)).astype(jnp.float32)
    cosines = jnp.cos(2.0 * jnp.pi / PERIOD * offsets)
    eps_list = [permittivity * (1.0 + cell_depth * cosines[level]) for level in range(STEPS)]
    forcings = []
    field_u = start_u
    field_v = start_v
    for level in range(STEPS):
        padded = padded_2(field_u, (("strip", 0),), STENCIL)
        forcing = laplacian_rows(padded, STENCIL) - damping_rate * field_v
        forcings.append(forcing)
        field_v = field_v + time_step * forcing / eps_list[level]
        field_u = field_u + time_step * field_v
    following = from_behind(jnp.stack([start_u, start_v]), "tm", -1)
    mismatch = jnp.stack([field_u, field_v]) - following
    retain = jnp.exp(-coarse_rate[0] / slice_count)
    ones = jnp.ones_like(retain)
    zeros = jnp.zeros_like(mismatch)
    higher_a, higher_b = entering((retain, mismatch), "tm", compose_high, (ones, zeros), True)
    lower_a, lower_b = entering((retain, mismatch), "tm", compose_low, (ones, zeros), False)
    cycle_a = retain * higher_a * lower_a
    cycle_b = retain[None] * (higher_a[None] * lower_b + higher_b) + mismatch
    coarse = cycle_b / (1.0 - cycle_a)[None]
    preceding = from_behind(coarse, "tm", 1)
    gradient_cells = jnp.zeros_like(start_u)
    back_u = coarse[0]
    back_v = coarse[1]
    for level in reversed(range(STEPS)):
        eps_now = eps_list[level]
        total_v = back_v + time_step * back_u
        weighted = time_step / eps_now * total_v
        padded = padded_2(weighted, (("strip", 0),), STENCIL)
        back_u = back_u + laplacian_rows(padded, STENCIL)
        back_v = (1.0 - time_step * damping_rate / eps_now) * total_v
        gradient_cells = gradient_cells - cosines[level] * time_step * total_v * forcings[level] / (
            eps_now * eps_now
        )
    cell_terms = gradient_cells * permittivity
    column_sums = jnp.sum(cell_terms.reshape(strip_rows, cell_terms.shape[1] // TILE, TILE), axis=2)
    selector = row_selector(strip_place * strip_rows, strip_rows, tile_map.shape[0])
    tile_part = jnp.dot(selector.T, column_sums, precision=lax.Precision.HIGHEST)
    param_part = jnp.sum(selector_params * tile_part[:, :, None], axis=(0, 1))
    depth_grad = lax.psum(param_part, ("tm", "strip"))
    adjoint_u = back_u - preceding[0]
    adjoint_v = back_v - preceding[1]
    return (adjoint_u[None], adjoint_v[None], depth_grad)


def solution(mesh):
    placed = (
        P("tm", "strip", None),
        P("tm", "strip", None),
        P("strip", None),
        P("tm", "strip", None),
        P(),
        P(),
        P("tm"),
    )
    return jax.shard_map(
        shards,
        mesh=mesh,
        in_specs=placed,
        out_specs=(P("tm", "strip", None), P("tm", "strip", None), P()),
        check_vma=False,
    )
```

profile of v0, /device:TPU:0, one launch (start us, length us, event | category | flops | bytes accessed | tf_op | source)
XLA Modules:
  0.0 250.6 jit_solution(9343302233114372609)
XLA Ops:
  7.2 1.8 fusion.108
  9.9 4.9 %collective-permute-start.1 = (f32[4,1024]{1,0:T(4,128)S(1)}, f32[4,1024]{1,0:T(4,128)S(1)}, u32[]{:S(2)}, u32[]{:S(2)}) collective-permute-start(f32[4,1024]{1,0:T(4,128)S(1)} %get-tuple-element.229), channel_id=1, source_target_pairs={{0,1},{2,3},{4,5},{6,7},{8,9},{10,11},{12,13},{14,15},{16,17},{18,... | collective-permute-start | bytes 49160 | tf_op jit(solution)/shard_map/ppermute | solution.py:23
  14.7 1.3 collective-permute-start
  16.0 1.9 pad_maximum_fusion
  17.9 3.7 %collective-permute-start.4 = (f32[2,64,1024]{2,1,0:T(8,128)}, f32[2,64,1024]{2,1,0:T(8,128)S(1)}, u32[]{:S(2)}, u32[]{:S(2)}) collective-permute-start(f32[2,64,1024]{2,1,0:T(8,128)} %pad_maximum_fusion), channel_id=1, source_target_pairs={{0,30},{2,0},{4,2},{6,4},{8,6},{10,8},{12,10},{14,12},{16,14},{18,... | collective-permute-start | bytes 1572872 | tf_op jit(solution)/shard_map/ppermute | solution.py:34
  27.2 1.2 fusion.148
  28.4 1.2 fusion.146
  29.5 1.2 fusion.144
  30.7 1.2 fusion.142
  31.9 1.3 fusion.99
  33.5 4.0 %multiply_add_fusion.1 = (f32[64,1024]{1,0:T(8,128)S(1)}, f32[64,1024]{1,0:T(8,128)S(1)}, f32[64,1024]{1,0:T(8,128)}, f32[64,1024]{1,0:T(8,128)S(1)}) fusion(f32[1,64,1024]{2,1,0:T(8,128)} %param.11, f32[1,64,1024]{2,1,0:T(8,128)} %param.12, f32[64,4]{1,0:T(8,128)S(1)} %get-tuple-element.231, f32[64,1020]{1,0:T(8,128)S(1)} %get-tuple-element.233, ...), kind=kLoop, calls=%fused_computation.193 | loop fusion | flops 2949120 | bytes 4489216 | tf_op jit(solution)/shard_map/add | solution.py:111
  37.5 4.3 %collective-permute-start.3 = (f32[4,1024]{1,0:T(4,128)S(1)}, f32[4,1024]{1,0:T(4,128)S(1)}, u32[]{:S(2)}, u32[]{:S(2)}) collective-permute-start(f32[4,1024]{1,0:T(4,128)S(1)} %get-tuple-element.211), channel_id=1, source_target_pairs={{0,1},{2,3},{4,5},{6,7},{8,9},{10,11},{12,13},{14,15},{16,17},{18,... | collective-permute-start | bytes 49160 | tf_op jit(solution)/shard_map/ppermute | solution.py:23
  41.8 1.3 collective-permute-start.2
  43.9 3.5 %collective-permute-done.2 = f32[4,1024]{1,0:T(4,128)S(1)} collective-permute-done((f32[4,1024]{1,0:T(4,128)S(1)}, f32[4,1024]{1,0:T(4,128)S(1)}, u32[]{:S(2)}, u32[]{:S(2)}) %collective-permute-start.2) | collective-permute-done | bytes 16416 | tf_op jit(solution)/shard_map/ppermute | solution.py:25
  50.4 15.8 %all-gather.4.cloned.1.call-done = f32[16,64,1024]{2,1,0:T(8,128)} async-done(((f32[1,64,1024]{2,1,0:T(8,128)}), f32[16,64,1024]{2,1,0:T(8,128)}) %all-gather.4.cloned.1.call-update) | async-done | bytes 4194320 | tf_op jit(solution)/shard_map/all_gather | solution.py:41
  66.2 75.0 %all-gather.6.cloned.1.call-done = f32[32,64,1024]{2,1,0:T(8,128)} async-done(((f32[2,64,1024]{2,1,0:T(8,128)}), f32[32,64,1024]{2,1,0:T(8,128)}) %all-gather.6.cloned.1.call-update) | async-done | bytes 8388624 | tf_op jit(solution)/shard_map/all_gather | solution.py:41
  141.3 35.1 %while.26 = (s32[]{:T(128)}, f32[64,1024]{1,0:T(8,128)S(1)}, f32[2,64,1024]{2,1,0:T(8,128)S(1)}, s32[]{:T(128)}, f32[16,64,1024]{2,1,0:T(8,128)}, /*index=5*/f32...) while((s32[]{:T(128)}, f32[64,1024]{1,0:T(8,128)S(1)}, f32[2,64,1024]{2,1,0:T(8,128)S(1)}, ...), condition=%wide.region_2.3_spmd, body=%wide.region_1.2_spmd.sunk | while | flops 327686 | bytes 2883747 | solution.py:50
  141.3 1.0 fusion.153
  142.3 1.3 bitcast_add_fusion.4
  143.7 1.0 fusion.153
  144.7 1.3 bitcast_add_fusion.4
  146.0 1.0 fusion.153
  147.0 1.3 bitcast_add_fusion.4
  148.3 1.0 fusion.153
  149.4 1.3 bitcast_add_fusion.4
  150.7 1.0 fusion.153
  151.7 1.3 bitcast_add_fusion.4
  153.0 1.0 fusion.153
  154.0 1.3 bitcast_add_fusion.4
  156.4 1.3 bitcast_add_fusion.4
  158.7 1.3 bitcast_add_fusion.4
  161.1 1.3 bitcast_add_fusion.4
  163.4 1.3 bitcast_add_fusion.4
  165.7 1.3 bitcast_add_fusion.4
  168.1 1.3 bitcast_add_fusion.4
  170.4 1.3 bitcast_add_fusion.4
  172.7 1.3 bitcast_add_fusion.4
  175.1 1.3 bitcast_add_fusion.4
  177.4 1.4 add_divide_fusion
  179.7 3.4 %collective-permute-start.6 = (f32[4,1024]{1,0:T(4,128)S(1)}, f32[4,1024]{1,0:T(4,128)S(1)}, u32[]{:S(2)}, u32[]{:S(2)}) collective-permute-start(f32[4,1024]{1,0:T(4,128)S(1)} %get-tuple-element.191), channel_id=1, source_target_pairs={{0,1},{2,3},{4,5},{6,7},{8,9},{10,11},{12,13},{14,15},{16,17},{18,... | collective-permute-start | bytes 49160 | tf_op jit(solution)/shard_map/ppermute | solution.py:23
  183.0 1.3 collective-permute-start.5
  184.5 4.2 %collective-permute-done.5 = f32[4,1024]{1,0:T(4,128)S(1)} collective-permute-done((f32[4,1024]{1,0:T(4,128)S(1)}, f32[4,1024]{1,0:T(4,128)S(1)}, u32[]{:S(2)}, u32[]{:S(2)}) %collective-permute-start.5) | collective-permute-done | bytes 16416 | tf_op jit(solution)/shard_map/ppermute | solution.py:25
  189.8 39.4 %psum.7 = f32[32]{0:T(128)} all-reduce(f32[32]{0:T(128)S(1)} %select_reduce_fusion), channel_id=1, replica_groups=mesh['tm'=16,'strip'=2] {'tm','strip'}, use_global_device_ids=true, to_apply=%region_7.8 | all-reduce | flops 32 | bytes 256 | tf_op jit(solution)/shard_map/psum | solution.py:141
  229.2 1.7 fusion.84
  231.7 4.2 %collective-permute-start.8 = (f32[4,1024]{1,0:T(4,128)S(1)}, f32[4,1024]{1,0:T(4,128)S(1)}, u32[]{:S(2)}, u32[]{:S(2)}) collective-permute-start(f32[4,1024]{1,0:T(4,128)S(1)} %get-tuple-element.177), channel_id=1, source_target_pairs={{0,1},{2,3},{4,5},{6,7},{8,9},{10,11},{12,13},{14,15},{16,17},{18,... | collective-permute-start | bytes 49160 | tf_op jit(solution)/shard_map/ppermute | solution.py:23
  235.9 1.3 collective-permute-start.7
  237.3 4.2 %collective-permute-done.7 = f32[4,1024]{1,0:T(4,128)S(1)} collective-permute-done((f32[4,1024]{1,0:T(4,128)S(1)}, f32[4,1024]{1,0:T(4,128)S(1)}, u32[]{:S(2)}, u32[]{:S(2)}) %collective-permute-start.7) | collective-permute-done | bytes 16416 | tf_op jit(solution)/shard_map/ppermute | solution.py:25
  241.5 2.2 fusion.9
  (86 shorter events, 21.8 us)
Async XLA Ops:
  7.2 59.0 %all-gather.4.cloned.1.call-start = ((), (), s32[]{:S(2)}) async-start(), calls=%async_computation | async-start | bytes 4456448 | tf_op jit(solution)/shard_map/all_gather | solution.py:41
  9.0 38.5 %copy-start = (f32[64,1024]{1,0:T(8,128)S(1)}, f32[64,1024]{1,0:T(8,128)}, u32[]{:S(2)}) copy-start(f32[64,1024]{1,0:T(8,128)} %param.13) | copy-start | bytes 786436
  9.0 132.2 %all-gather.6.cloned.1.call-start = ((), (), s32[]{:S(2)}) async-start(), calls=%async_computation.1 | async-start | bytes 8912896 | tf_op jit(solution)/shard_map/all_gather | solution.py:41
  9.9 23.5 %collective-permute-start.1 = (f32[4,1024]{1,0:T(4,128)S(1)}, f32[4,1024]{1,0:T(4,128)S(1)}, u32[]{:S(2)}, u32[]{:S(2)}) collective-permute-start(f32[4,1024]{1,0:T(4,128)S(1)} %get-tuple-element.229), channel_id=1, source_target_pairs={{0,1},{2,3},{4,5},{6,7},{8,9},{10,11},{12,13},{14,15},{16,17},{18,... | collective-permute-start | bytes 49160 | tf_op jit(solution)/shard_map/ppermute | solution.py:23
  14.7 18.6 %collective-permute-start = (f32[4,1024]{1,0:T(4,128)S(1)}, f32[4,1024]{1,0:T(4,128)S(1)}, u32[]{:S(2)}, u32[]{:S(2)}) collective-permute-start(f32[4,1024]{1,0:T(4,128)S(1)} %get-tuple-element.228), channel_id=1, source_target_pairs={{1,0},{3,2},{5,4},{7,6},{9,8},{11,10},{13,12},{15,14},{17,16},{19,... | collective-permute-start | bytes 49160 | tf_op jit(solution)/shard_map/ppermute | solution.py:25
  17.9 30.3 %collective-permute-start.4 = (f32[2,64,1024]{2,1,0:T(8,128)}, f32[2,64,1024]{2,1,0:T(8,128)S(1)}, u32[]{:S(2)}, u32[]{:S(2)}) collective-permute-start(f32[2,64,1024]{2,1,0:T(8,128)} %pad_maximum_fusion), channel_id=1, source_target_pairs={{0,30},{2,0},{4,2},{6,4},{8,6},{10,8},{12,10},{14,12},{16,14},{18,... | collective-permute-start | bytes 1572872 | tf_op jit(solution)/shard_map/ppermute | solution.py:34
  37.5 6.4 %collective-permute-start.3 = (f32[4,1024]{1,0:T(4,128)S(1)}, f32[4,1024]{1,0:T(4,128)S(1)}, u32[]{:S(2)}, u32[]{:S(2)}) collective-permute-start(f32[4,1024]{1,0:T(4,128)S(1)} %get-tuple-element.211), channel_id=1, source_target_pairs={{0,1},{2,3},{4,5},{6,7},{8,9},{10,11},{12,13},{14,15},{16,17},{18,... | collective-permute-start | bytes 49160 | tf_op jit(solution)/shard_map/ppermute | solution.py:23
  41.8 5.6 %collective-permute-start.2 = (f32[4,1024]{1,0:T(4,128)S(1)}, f32[4,1024]{1,0:T(4,128)S(1)}, u32[]{:S(2)}, u32[]{:S(2)}) collective-permute-start(f32[4,1024]{1,0:T(4,128)S(1)} %get-tuple-element.210), channel_id=1, source_target_pairs={{1,0},{3,2},{5,4},{7,6},{9,8},{11,10},{13,12},{15,14},{17,16},{19,... | collective-permute-start | bytes 49160 | tf_op jit(solution)/shard_map/ppermute | solution.py:25
  48.2 93.0 %copy-start.1 = (f32[2,64,1024]{2,1,0:T(8,128)}, f32[2,64,1024]{2,1,0:T(8,128)S(1)}, u32[]{:S(2)}) copy-start(f32[2,64,1024]{2,1,0:T(8,128)S(1)} %collective-permute-done.4) | copy-start | bytes 1572868
  176.4 1.0 copy-start.3
  176.5 12.2 %copy-start.2 = (f32[64,1024]{1,0:T(8,128)S(1)}, f32[64,1024]{1,0:T(8,128)}, u32[]{:S(2)}) copy-start(f32[64,1024]{1,0:T(8,128)} %get-tuple-element.156) | copy-start | bytes 786436
  176.5 13.2 %copy-start.4 = (s32[1,8]{1,0:T(1,128)S(1)}, s32[1,8]{1,0:T(1,128)}, u32[]{:S(2)}) copy-start(s32[1,8]{1,0:T(1,128)} %param.16) | copy-start | bytes 100
  179.7 4.8 %collective-permute-start.6 = (f32[4,1024]{1,0:T(4,128)S(1)}, f32[4,1024]{1,0:T(4,128)S(1)}, u32[]{:S(2)}, u32[]{:S(2)}) collective-permute-start(f32[4,1024]{1,0:T(4,128)S(1)} %get-tuple-element.191), channel_id=1, source_target_pairs={{0,1},{2,3},{4,5},{6,7},{8,9},{10,11},{12,13},{14,15},{16,17},{18,... | collective-permute-start | bytes 49160 | tf_op jit(solution)/shard_map/ppermute | solution.py:23
  183.0 5.6 %collective-permute-start.5 = (f32[4,1024]{1,0:T(4,128)S(1)}, f32[4,1024]{1,0:T(4,128)S(1)}, u32[]{:S(2)}, u32[]{:S(2)}) collective-permute-start(f32[4,1024]{1,0:T(4,128)S(1)} %get-tuple-element.190), channel_id=1, source_target_pairs={{1,0},{3,2},{5,4},{7,6},{9,8},{11,10},{13,12},{15,14},{17,16},{19,... | collective-permute-start | bytes 49160 | tf_op jit(solution)/shard_map/ppermute | solution.py:25
  184.4 44.8 %collective-permute-start.9 = (f32[2,64,1024]{2,1,0:T(8,128)S(1)}, f32[2,64,1024]{2,1,0:T(8,128)}, u32[]{:S(2)}, u32[]{:S(2)}) collective-permute-start(f32[2,64,1024]{2,1,0:T(8,128)S(1)} %add_divide_fusion), channel_id=1, source_target_pairs={{0,2},{2,4},{4,6},{6,8},{8,10},{10,12},{12,14},{14,16},{16,18},{18... | collective-permute-start | bytes 1572872 | tf_op jit(solution)/shard_map/ppermute | solution.py:34
  231.7 5.6 %collective-permute-start.8 = (f32[4,1024]{1,0:T(4,128)S(1)}, f32[4,1024]{1,0:T(4,128)S(1)}, u32[]{:S(2)}, u32[]{:S(2)}) collective-permute-start(f32[4,1024]{1,0:T(4,128)S(1)} %get-tuple-element.177), channel_id=1, source_target_pairs={{0,1},{2,3},{4,5},{6,7},{8,9},{10,11},{12,13},{14,15},{16,17},{18,... | collective-permute-start | bytes 49160 | tf_op jit(solution)/shard_map/ppermute | solution.py:23
  235.9 5.6 %collective-permute-start.7 = (f32[4,1024]{1,0:T(4,128)S(1)}, f32[4,1024]{1,0:T(4,128)S(1)}, u32[]{:S(2)}, u32[]{:S(2)}) collective-permute-start(f32[4,1024]{1,0:T(4,128)S(1)} %get-tuple-element.176), channel_id=1, source_target_pairs={{1,0},{3,2},{5,4},{7,6},{9,8},{11,10},{13,12},{15,14},{17,16},{19,... | collective-permute-start | bytes 49160 | tf_op jit(solution)/shard_map/ppermute | solution.py:25
Sparse Core Ops, SparseCore 0:
  10.1 56.0 all-gather.3
  68.4 72.8 all-gather.5
where the time goes:
time: 253 us; the launch traced here: 251 us
  waiting for transfers between devices  103 us (41%)
  other arithmetic  52.5 us (21%)
  blocking collectives  39.4 us (16%)
  starting transfers between devices  25.6 us (10%)
  between operations  16.3 us (6%)
  local copies, waits for them, and re-layouts  13.4 us (5%)
    all_gather x2, waiting for transfers between devices, entering(): gathered = jax.tree.map(lambda a: lax.all_gather(a, axis), part)  90.8 us
    psum x1, blocking collectives, shards(): depth_grad = lax.psum(param_part, ('tm', 'strip'))  39.4 us
    add x15, other arithmetic, compose_high(): return (latter[0] * earlier[0], latter[0][None] * earlier[1] + latter[1])  19.3 us
    ppermute x4, starting transfers between devices, padded_2(): lax.ppermute(tail, axis, [(i, (i + 1) % count) for i in range(ends)])  16.7 us
    mul x15, other arithmetic, compose_high(): return (latter[0] * earlier[0], latter[0][None] * earlier[1] + latter[1])  15.4 us
    ppermute x4, waiting for transfers between devices, padded_2(): lax.ppermute(head, axis, [((i + 1) % count, i) for i in range(ends)])  11.9 us
    slice x24, local copies, waits for them, and re-layouts, laplacian_rows(): jnp.roll(center, offset, axis=1) + jnp.roll(center, -offset, axis=1)  9.75 us
    ppermute x4, starting transfers between devices, padded_2(): lax.ppermute(head, axis, [((i + 1) % count, i) for i in range(ends)])  5.17 us
  transfers between devices with their start and end apart: 12, of which 5 were waited for; matrix products, arithmetic and copies ran while one was open for 9% of the time, Pallas kernels for 0%

commit v1 on v0

--- a/solution.py
+++ b/solution.py
@@ -138,7 +138,7 @@
     selector = row_selector(strip_place * strip_rows, strip_rows, tile_map.shape[0])
     tile_part = jnp.dot(selector.T, column_sums, precision=lax.Precision.HIGHEST)
     param_part = jnp.sum(selector_params * tile_part[:, :, None], axis=(0, 1))
-    depth_grad = lax.psum(param_part, ("tm", "strip"))
+    depth_grad = lax.psum(lax.psum(param_part, "tm"), "strip")
     adjoint_u = back_u - preceding[0]
     adjoint_v = back_v - preceding[1]
     return (adjoint_u[None], adjoint_v[None], depth_grad)

time: 253 us -> 249 us (0.984)
  blocking collectives: 39.4 us -> 35.7 us
    psum x1 -> x2, blocking collectives: 39.4 us -> 35.7 us  [shards(): depth_grad = lax.psum(lax.psum(param_part, 'tm'), 'strip')]
where the time goes in v1:
time: 249 us; the launch traced here: 247 us
  waiting for transfers between devices  103 us (41%)
  other arithmetic  52.5 us (21%)
  blocking collectives  35.7 us (14%)
  starting transfers between devices  25.4 us (10%)
  between operations  16.3 us (7%)
  local copies, waits for them, and re-layouts  13.4 us (5%)
    all_gather x2, waiting for transfers between devices, entering(): gathered = jax.tree.map(lambda a: lax.all_gather(a, axis), part)  90.8 us
    psum x2, blocking collectives, shards(): depth_grad = lax.psum(lax.psum(param_part, 'tm'), 'strip')  35.7 us
    add x15, other arithmetic, compose_high(): return (latter[0] * earlier[0], latter[0][None] * earlier[1] + latter[1])  19.3 us
    ppermute x4, starting transfers between devices, padded_2(): lax.ppermute(tail, axis, [(i, (i + 1) % count) for i in range(ends)])  16.4 us
    mul x15, other arithmetic, compose_high(): return (latter[0] * earlier[0], latter[0][None] * earlier[1] + latter[1])  15.4 us
    ppermute x4, waiting for transfers between devices, padded_2(): lax.ppermute(head, axis, [((i + 1) % count, i) for i in range(ends)])  11.9 us
    slice x24, local copies, waits for them, and re-layouts, laplacian_rows(): jnp.roll(center, offset, axis=1) + jnp.roll(center, -offset, axis=1)  9.75 us
    ppermute x4, starting transfers between devices, padded_2(): lax.ppermute(head, axis, [((i + 1) % count, i) for i in range(ends)])  5.17 us
  transfers between devices with their start and end apart: 12, of which 5 were waited for; matrix products, arithmetic and copies ran while one was open for 9% of the time, Pallas kernels for 0%

profile of v1, /device:TPU:0, one launch (start us, length us, event | category | flops | bytes accessed | tf_op | source)
XLA Modules:
  0.0 246.6 jit_solution(18319678654627542253)
XLA Ops:
  7.2 1.8 fusion.108
  9.9 4.9 %collective-permute-start.1 = (f32[4,1024]{1,0:T(4,128)S(1)}, f32[4,1024]{1,0:T(4,128)S(1)}, u32[]{:S(2)}, u32[]{:S(2)}) collective-permute-start(f32[4,1024]{1,0:T(4,128)S(1)} %get-tuple-element.229), channel_id=1, source_target_pairs={{0,1},{2,3},{4,5},{6,7},{8,9},{10,11},{12,13},{14,15},{16,17},{18,... | collective-permute-start | bytes 49160 | tf_op jit(solution)/shard_map/ppermute | solution.py:23
  14.7 1.3 collective-permute-start
  16.0 1.9 pad_maximum_fusion
  17.9 3.7 %collective-permute-start.4 = (f32[2,64,1024]{2,1,0:T(8,128)}, f32[2,64,1024]{2,1,0:T(8,128)S(1)}, u32[]{:S(2)}, u32[]{:S(2)}) collective-permute-start(f32[2,64,1024]{2,1,0:T(8,128)} %pad_maximum_fusion), channel_id=1, source_target_pairs={{0,30},{2,0},{4,2},{6,4},{8,6},{10,8},{12,10},{14,12},{16,14},{18,... | collective-permute-start | bytes 1572872 | tf_op jit(solution)/shard_map/ppermute | solution.py:34
  27.2 1.2 fusion.148
  28.4 1.2 fusion.146
  29.5 1.2 fusion.144
  30.7 1.2 fusion.142
  31.9 1.3 fusion.99
  33.5 4.0 %multiply_add_fusion.1 = (f32[64,1024]{1,0:T(8,128)S(1)}, f32[64,1024]{1,0:T(8,128)S(1)}, f32[64,1024]{1,0:T(8,128)}, f32[64,1024]{1,0:T(8,128)S(1)}) fusion(f32[1,64,1024]{2,1,0:T(8,128)} %param.11, f32[1,64,1024]{2,1,0:T(8,128)} %param.12, f32[64,4]{1,0:T(8,128)S(1)} %get-tuple-element.231, f32[64,1020]{1,0:T(8,128)S(1)} %get-tuple-element.233, ...), kind=kLoop, calls=%fused_computation.193 | loop fusion | flops 2949120 | bytes 4489216 | tf_op jit(solution)/shard_map/add | solution.py:111
  37.5 4.3 %collective-permute-start.3 = (f32[4,1024]{1,0:T(4,128)S(1)}, f32[4,1024]{1,0:T(4,128)S(1)}, u32[]{:S(2)}, u32[]{:S(2)}) collective-permute-start(f32[4,1024]{1,0:T(4,128)S(1)} %get-tuple-element.211), channel_id=1, source_target_pairs={{0,1},{2,3},{4,5},{6,7},{8,9},{10,11},{12,13},{14,15},{16,17},{18,... | collective-permute-start | bytes 49160 | tf_op jit(solution)/shard_map/ppermute | solution.py:23
  41.8 1.3 collective-permute-start.2
  44.0 3.5 %collective-permute-done.2 = f32[4,1024]{1,0:T(4,128)S(1)} collective-permute-done((f32[4,1024]{1,0:T(4,128)S(1)}, f32[4,1024]{1,0:T(4,128)S(1)}, u32[]{:S(2)}, u32[]{:S(2)}) %collective-permute-start.2) | collective-permute-done | bytes 16416 | tf_op jit(solution)/shard_map/ppermute | solution.py:25
  50.4 15.8 %all-gather.4.cloned.1.call-done = f32[16,64,1024]{2,1,0:T(8,128)} async-done(((f32[1,64,1024]{2,1,0:T(8,128)}), f32[16,64,1024]{2,1,0:T(8,128)}) %all-gather.4.cloned.1.call-update) | async-done | bytes 4194320 | tf_op jit(solution)/shard_map/all_gather | solution.py:41
  66.2 75.0 %all-gather.6.cloned.1.call-done = f32[32,64,1024]{2,1,0:T(8,128)} async-done(((f32[2,64,1024]{2,1,0:T(8,128)}), f32[32,64,1024]{2,1,0:T(8,128)}) %all-gather.6.cloned.1.call-update) | async-done | bytes 8388624 | tf_op jit(solution)/shard_map/all_gather | solution.py:41
  141.3 35.1 %while.26 = (s32[]{:T(128)}, f32[64,1024]{1,0:T(8,128)S(1)}, f32[2,64,1024]{2,1,0:T(8,128)S(1)}, s32[]{:T(128)}, f32[16,64,1024]{2,1,0:T(8,128)}, /*index=5*/f32...) while((s32[]{:T(128)}, f32[64,1024]{1,0:T(8,128)S(1)}, f32[2,64,1024]{2,1,0:T(8,128)S(1)}, ...), condition=%wide.region_2.3_spmd, body=%wide.region_1.2_spmd.sunk | while | flops 327686 | bytes 2883747 | solution.py:50
  141.3 1.0 fusion.153
  142.4 1.3 bitcast_add_fusion.4
  143.7 1.0 fusion.153
  144.7 1.3 bitcast_add_fusion.4
  146.0 1.0 fusion.153
  147.0 1.3 bitcast_add_fusion.4
  148.3 1.0 fusion.153
  149.4 1.3 bitcast_add_fusion.4
  150.7 1.0 fusion.153
  151.7 1.3 bitcast_add_fusion.4
  154.0 1.3 bitcast_add_fusion.4
  156.4 1.3 bitcast_add_fusion.4
  158.7 1.3 bitcast_add_fusion.4
  161.1 1.3 bitcast_add_fusion.4
  163.4 1.3 bitcast_add_fusion.4
  165.7 1.3 bitcast_add_fusion.4
  168.1 1.3 bitcast_add_fusion.4
  170.4 1.3 bitcast_add_fusion.4
  172.8 1.3 bitcast_add_fusion.4
  175.1 1.3 bitcast_add_fusion.4
  177.4 1.4 add_divide_fusion
  179.7 3.4 %collective-permute-start.6 = (f32[4,1024]{1,0:T(4,128)S(1)}, f32[4,1024]{1,0:T(4,128)S(1)}, u32[]{:S(2)}, u32[]{:S(2)}) collective-permute-start(f32[4,1024]{1,0:T(4,128)S(1)} %get-tuple-element.191), channel_id=1, source_target_pairs={{0,1},{2,3},{4,5},{6,7},{8,9},{10,11},{12,13},{14,15},{16,17},{18,... | collective-permute-start | bytes 49160 | tf_op jit(solution)/shard_map/ppermute | solution.py:23
  183.1 1.3 collective-permute-start.5
  184.5 4.2 %collective-permute-done.5 = f32[4,1024]{1,0:T(4,128)S(1)} collective-permute-done((f32[4,1024]{1,0:T(4,128)S(1)}, f32[4,1024]{1,0:T(4,128)S(1)}, u32[]{:S(2)}, u32[]{:S(2)}) %collective-permute-start.5) | collective-permute-done | bytes 16416 | tf_op jit(solution)/shard_map/ppermute | solution.py:25
  189.8 29.7 %psum.14 = f32[32]{0:T(128)S(1)} all-reduce(f32[32]{0:T(128)S(1)} %select_reduce_fusion), channel_id=1, replica_groups=mesh['tm'=16,'strip'=2] {'tm'}, use_global_device_ids=true, to_apply=%region_7.8 | all-reduce | flops 32 | bytes 256 | tf_op jit(solution)/shard_map/psum | solution.py:141
  219.5 6.0 %psum.15 = f32[32]{0:T(128)} all-reduce(f32[32]{0:T(128)S(1)} %psum.14), channel_id=1, replica_groups=mesh['tm'=16,'strip'=2] {'strip'}, use_global_device_ids=true, to_apply=%region_8.9 | all-reduce | flops 32 | bytes 256 | tf_op jit(solution)/shard_map/psum | solution.py:141
  225.5 1.7 fusion.84
  228.0 3.9 %collective-permute-start.8 = (f32[4,1024]{1,0:T(4,128)S(1)}, f32[4,1024]{1,0:T(4,128)S(1)}, u32[]{:S(2)}, u32[]{:S(2)}) collective-permute-start(f32[4,1024]{1,0:T(4,128)S(1)} %get-tuple-element.177), channel_id=1, source_target_pairs={{0,1},{2,3},{4,5},{6,7},{8,9},{10,11},{12,13},{14,15},{16,17},{18,... | collective-permute-start | bytes 49160 | tf_op jit(solution)/shard_map/ppermute | solution.py:23
  232.0 1.3 collective-permute-start.7
  233.4 4.2 %collective-permute-done.7 = f32[4,1024]{1,0:T(4,128)S(1)} collective-permute-done((f32[4,1024]{1,0:T(4,128)S(1)}, f32[4,1024]{1,0:T(4,128)S(1)}, u32[]{:S(2)}, u32[]{:S(2)}) %collective-permute-start.7) | collective-permute-done | bytes 16416 | tf_op jit(solution)/shard_map/ppermute | solution.py:25
  237.6 2.2 fusion.9
  (87 shorter events, 22.8 us)
Async XLA Ops:
  7.2 59.0 %all-gather.4.cloned.1.call-start = ((), (), s32[]{:S(2)}) async-start(), calls=%async_computation | async-start | bytes 4456448 | tf_op jit(solution)/shard_map/all_gather | solution.py:41
  9.0 38.5 %copy-start = (f32[64,1024]{1,0:T(8,128)S(1)}, f32[64,1024]{1,0:T(8,128)}, u32[]{:S(2)}) copy-start(f32[64,1024]{1,0:T(8,128)} %param.13) | copy-start | bytes 786436
  9.0 132.2 %all-gather.6.cloned.1.call-start = ((), (), s32[]{:S(2)}) async-start(), calls=%async_computation.1 | async-start | bytes 8912896 | tf_op jit(solution)/shard_map/all_gather | solution.py:41
  9.9 23.5 %collective-permute-start.1 = (f32[4,1024]{1,0:T(4,128)S(1)}, f32[4,1024]{1,0:T(4,128)S(1)}, u32[]{:S(2)}, u32[]{:S(2)}) collective-permute-start(f32[4,1024]{1,0:T(4,128)S(1)} %get-tuple-element.229), channel_id=1, source_target_pairs={{0,1},{2,3},{4,5},{6,7},{8,9},{10,11},{12,13},{14,15},{16,17},{18,... | collective-permute-start | bytes 49160 | tf_op jit(solution)/shard_map/ppermute | solution.py:23
  14.7 18.7 %collective-permute-start = (f32[4,1024]{1,0:T(4,128)S(1)}, f32[4,1024]{1,0:T(4,128)S(1)}, u32[]{:S(2)}, u32[]{:S(2)}) collective-permute-start(f32[4,1024]{1,0:T(4,128)S(1)} %get-tuple-element.228), channel_id=1, source_target_pairs={{1,0},{3,2},{5,4},{7,6},{9,8},{11,10},{13,12},{15,14},{17,16},{19,... | collective-permute-start | bytes 49160 | tf_op jit(solution)/shard_map/ppermute | solution.py:25
  17.9 30.3 %collective-permute-start.4 = (f32[2,64,1024]{2,1,0:T(8,128)}, f32[2,64,1024]{2,1,0:T(8,128)S(1)}, u32[]{:S(2)}, u32[]{:S(2)}) collective-permute-start(f32[2,64,1024]{2,1,0:T(8,128)} %pad_maximum_fusion), channel_id=1, source_target_pairs={{0,30},{2,0},{4,2},{6,4},{8,6},{10,8},{12,10},{14,12},{16,14},{18,... | collective-permute-start | bytes 1572872 | tf_op jit(solution)/shard_map/ppermute | solution.py:34
  37.5 6.4 %collective-permute-start.3 = (f32[4,1024]{1,0:T(4,128)S(1)}, f32[4,1024]{1,0:T(4,128)S(1)}, u32[]{:S(2)}, u32[]{:S(2)}) collective-permute-start(f32[4,1024]{1,0:T(4,128)S(1)} %get-tuple-element.211), channel_id=1, source_target_pairs={{0,1},{2,3},{4,5},{6,7},{8,9},{10,11},{12,13},{14,15},{16,17},{18,... | collective-permute-start | bytes 49160 | tf_op jit(solution)/shard_map/ppermute | solution.py:23
  41.8 5.6 %collective-permute-start.2 = (f32[4,1024]{1,0:T(4,128)S(1)}, f32[4,1024]{1,0:T(4,128)S(1)}, u32[]{:S(2)}, u32[]{:S(2)}) collective-permute-start(f32[4,1024]{1,0:T(4,128)S(1)} %get-tuple-element.210), channel_id=1, source_target_pairs={{1,0},{3,2},{5,4},{7,6},{9,8},{11,10},{13,12},{15,14},{17,16},{19,... | collective-permute-start | bytes 49160 | tf_op jit(solution)/shard_map/ppermute | solution.py:25
  48.2 93.0 %copy-start.1 = (f32[2,64,1024]{2,1,0:T(8,128)}, f32[2,64,1024]{2,1,0:T(8,128)S(1)}, u32[]{:S(2)}) copy-start(f32[2,64,1024]{2,1,0:T(8,128)S(1)} %collective-permute-done.4) | copy-start | bytes 1572868
  176.4 1.0 copy-start.3
  176.5 12.2 %copy-start.2 = (f32[64,1024]{1,0:T(8,128)S(1)}, f32[64,1024]{1,0:T(8,128)}, u32[]{:S(2)}) copy-start(f32[64,1024]{1,0:T(8,128)} %get-tuple-element.156) | copy-start | bytes 786436
  176.5 13.2 %copy-start.4 = (s32[1,8]{1,0:T(1,128)S(1)}, s32[1,8]{1,0:T(1,128)}, u32[]{:S(2)}) copy-start(s32[1,8]{1,0:T(1,128)} %param.16) | copy-start | bytes 100
  179.7 4.8 %collective-permute-start.6 = (f32[4,1024]{1,0:T(4,128)S(1)}, f32[4,1024]{1,0:T(4,128)S(1)}, u32[]{:S(2)}, u32[]{:S(2)}) collective-permute-start(f32[4,1024]{1,0:T(4,128)S(1)} %get-tuple-element.191), channel_id=1, source_target_pairs={{0,1},{2,3},{4,5},{6,7},{8,9},{10,11},{12,13},{14,15},{16,17},{18,... | collective-permute-start | bytes 49160 | tf_op jit(solution)/shard_map/ppermute | solution.py:23
  183.1 5.6 %collective-permute-start.5 = (f32[4,1024]{1,0:T(4,128)S(1)}, f32[4,1024]{1,0:T(4,128)S(1)}, u32[]{:S(2)}, u32[]{:S(2)}) collective-permute-start(f32[4,1024]{1,0:T(4,128)S(1)} %get-tuple-element.190), channel_id=1, source_target_pairs={{1,0},{3,2},{5,4},{7,6},{9,8},{11,10},{13,12},{15,14},{17,16},{19,... | collective-permute-start | bytes 49160 | tf_op jit(solution)/shard_map/ppermute | solution.py:25
  184.4 41.1 %collective-permute-start.9 = (f32[2,64,1024]{2,1,0:T(8,128)S(1)}, f32[2,64,1024]{2,1,0:T(8,128)}, u32[]{:S(2)}, u32[]{:S(2)}) collective-permute-start(f32[2,64,1024]{2,1,0:T(8,128)S(1)} %add_divide_fusion), channel_id=1, source_target_pairs={{0,2},{2,4},{4,6},{6,8},{8,10},{10,12},{12,14},{14,16},{16,18},{18... | collective-permute-start | bytes 1572872 | tf_op jit(solution)/shard_map/ppermute | solution.py:34
  228.0 5.4 %collective-permute-start.8 = (f32[4,1024]{1,0:T(4,128)S(1)}, f32[4,1024]{1,0:T(4,128)S(1)}, u32[]{:S(2)}, u32[]{:S(2)}) collective-permute-start(f32[4,1024]{1,0:T(4,128)S(1)} %get-tuple-element.177), channel_id=1, source_target_pairs={{0,1},{2,3},{4,5},{6,7},{8,9},{10,11},{12,13},{14,15},{16,17},{18,... | collective-permute-start | bytes 49160 | tf_op jit(solution)/shard_map/ppermute | solution.py:23
  232.0 5.6 %collective-permute-start.7 = (f32[4,1024]{1,0:T(4,128)S(1)}, f32[4,1024]{1,0:T(4,128)S(1)}, u32[]{:S(2)}, u32[]{:S(2)}) collective-permute-start(f32[4,1024]{1,0:T(4,128)S(1)} %get-tuple-element.176), channel_id=1, source_target_pairs={{1,0},{3,2},{5,4},{7,6},{9,8},{11,10},{13,12},{15,14},{17,16},{19,... | collective-permute-start | bytes 49160 | tf_op jit(solution)/shard_map/ppermute | solution.py:25
Sparse Core Ops, SparseCore 0:
  10.1 56.0 all-gather.3
  68.4 72.8 all-gather.5
